TPU v7x, 512 devices: a whole 4x8x8 slice. The times are simulated.
512 devices in a mesh: dof: 64 (over z, y_lo, core), real: 8 (over y_hi, x).
Axes of the slice: x: 4, y: 8 (y_hi: 2, y_lo: 4; y = y_hi * 4 + y_lo), z: 8, core: 2. Of those that a mesh axis runs over, the one named last changes fastest.
Arguments:
- mode_panel: bfloat16 [131072, 512], P('dof'), may hold values from -0.31445312 to 0.31445312
- stiff_blocks: bfloat16 [1024, 5, 128, 128], P('dof'), as said below
- stiff_cols: int32 [1024, 5], P('dof'), may hold values from 0 to 1023, as said below
- row_blade: int32 [131072], P('dof'), may hold values from 0 to 3, as said below
- adjusted_values: float32 [512], replicated, may hold values from 4 to 24
- deviations: float32 [128, 4], P('dof'), may hold values from -0.05 to 0.05
- start_block: float32 [512, 128], P('real'), may hold values from -6 to 6
Outputs:
- projected: float32 [4, 512, 512], P(None, 'real')
- subspace: float32 [128, 512, 128], P('dof', 'real')
Inputs may be any that keep to these rules, and one draw needn't show every extreme that they name: `stiff_cols`: each block row's 5 entries are, in some order, the block row itself and the block rows two and one before and one and two after it; where one of those lies outside the grid or in another blade's rows, the block row itself stands in. `stiff_blocks`: the stiffness is symmetric and couples no two blades: the block of block row g at column c is the transpose of the block of block row c at column g, diagonal blocks are symmetric, and stand-in blocks are zero. `row_blade`: block row g belongs to the blade numbered ((g + 8) // 256) mod 4 under a fixed relabelling of the blades; so each blade owns a run of 32768 neighbouring rows, except one blade, which owns the first 31744 rows and the last 1024 rows.
All inputs are finite; a program needn't handle non-finite values.
Results may differ from a plain program's by a relative error of at most 0.003.
Values may be sent and summed in bfloat16 or wider, within the bound.
No kernel may reach another device: no remote copies, remote signals or barrier semaphores. Data moves between devices by JAX's collectives and lax.ppermute only.
A program may use at most 64 MiB of HBM per device.

v0:
```python
import jax
import jax.numpy as jnp
from jax import lax
from jax.sharding import PartitionSpec as P

ADJUSTED_MODES = 512
NBLADE = 4
STEPS = 2
highest_accuracy = lax.Precision.HIGHEST


def with_halo(block, sides, width):
    for axis, dim in sides:
        count = lax.axis_size(axis)
        forward = [(i, i + 1) for i in range(count - 1)]
        backward = [(target, source) for source, target in forward]
        low = lax.ppermute(
            lax.slice_in_dim(block, block.shape[dim] - width, None, axis=dim), axis, forward
        )
        high = lax.ppermute(lax.slice_in_dim(block, 0, width, axis=dim), axis, backward)
        block = jnp.concatenate([low, block, high], axis=dim)
    return block


def multiply_by_blocks(ext_blocks, blocks, columns):
    number = blocks.shape[0]
    size = blocks.shape[2]
    mode_count = ext_blocks.shape[2]
    row_totals = jnp.zeros((number, size, mode_count), jnp.float32)
    for slot_index in range(blocks.shape[1]):
        picked = jnp.take(ext_blocks, columns[:, slot_index], axis=0)
        row_totals = row_totals + jnp.einsum(
            "gab,gbm->gam", blocks[:, slot_index], picked, preferred_element_type=jnp.float32
        )
    return row_totals.reshape(number * size, mode_count).astype(jnp.bfloat16)


def add_projection(portion, offset, mode_panel, row_blade, col_start, owned_rows):
    number = portion.shape[0]
    left_rows = lax.dynamic_slice(mode_panel, (offset, col_start), (number, owned_rows))
    stacked = jnp.concatenate(
        [
            jnp.where((row_blade == blade_index)[:, None], left_rows, jnp.zeros_like(left_rows))
            for blade_index in range(NBLADE)
        ],
        axis=1,
    )
    return lax.dot_general(
        stacked, portion, (((0,), (0,)), ((), ())), preferred_element_type=jnp.float32
    )


def inverse_factor(inner_product_matrix):
    factor = jnp.linalg.cholesky(inner_product_matrix)
    identity = jnp.broadcast_to(
        jnp.eye(inner_product_matrix.shape[-1], dtype=inner_product_matrix.dtype),
        inner_product_matrix.shape,
    )
    return lax.linalg.triangular_solve(factor, identity, left_side=True, lower=True)


def normalize_parts(present_image):
    partial_inner_products = jnp.einsum(
        "eox,eol->exl", present_image, present_image, precision=highest_accuracy
    )
    inner_product_matrix = lax.psum(partial_inner_products, "real") / ADJUSTED_MODES
    inverse = inverse_factor(inner_product_matrix)
    return jnp.einsum("zjs,zts->zjt", present_image, inverse, precision=highest_accuracy)


def on_device(
    mode_panel, stiff_blocks, stiff_cols, row_blade, adjusted_values, deviations, start_block
):
    real_count = lax.axis_size("real")
    owner_index = lax.axis_index("real")
    mode_count = mode_panel.shape[1]
    owned_rows = mode_count // real_count
    block_size = stiff_blocks.shape[2]
    shard_blocks = stiff_blocks.shape[0]
    col_start = owner_index * owned_rows
    extended = with_halo(mode_panel, (("dof", 0),), 2 * block_size)
    ext_blocks = extended.reshape(shard_blocks + 4, block_size, mode_count)
    local_cols = stiff_cols - lax.axis_index("dof") * shard_blocks + 2
    stiff_image = multiply_by_blocks(ext_blocks, stiff_blocks, local_cols)
    blade_parts = add_projection(
        stiff_image, jnp.zeros((), jnp.int32), mode_panel, row_blade, col_start, owned_rows
    )
    summed = lax.psum(blade_parts, "dof")
    projected = summed.reshape(NBLADE, owned_rows, mode_count)
    row_ids = jnp.arange(owned_rows, dtype=jnp.int32) + col_start
    own_values = lax.dynamic_slice_in_dim(adjusted_values, col_start, owned_rows, 0)
    diagonal_part = jnp.where(
        jnp.arange(mode_count, dtype=jnp.int32)[None, :] == row_ids[:, None],
        own_values[:, None],
        jnp.zeros((), jnp.float32),
    )
    realizations = deviations.shape[0]
    subspace_width = start_block.shape[1]
    reduced = (
        jnp.einsum("zb,bjm->zjm", deviations, projected, precision=highest_accuracy)
        + diagonal_part[None]
    )
    current = jnp.broadcast_to(start_block[None], (realizations, owned_rows, subspace_width))
    for iteration in range(STEPS):
        present_image = jnp.einsum(
            "zjk,zks->zjs",
            reduced,
            lax.all_gather(current, "real", axis=1, tiled=True),
            precision=highest_accuracy,
        )
        current = normalize_parts(present_image)
    return (projected, current)


def solution(mesh):
    in_specs = (
        P("dof", None),
        P("dof", None, None, None),
        P("dof", None),
        P("dof"),
        P(),
        P("dof", None),
        P("real", None),
    )
    out_specs = (P(None, "real", None), P("dof", "real", None))
    return jax.shard_map(
        on_device, mesh=mesh, in_specs=in_specs, out_specs=out_specs, check_vma=False
    )
```

profile of v0, /device:TPU:64, one launch (start us, length us, event | category | flops | bytes accessed | tf_op | source)
XLA Modules:
  0.0 967.4 jit_solution(17578840527042316968)
XLA Ops:
  7.2 1.1 fusion.60
  8.3 1.9 collective-permute-start
  10.2 6.3 collective-permute-start.1
  18.0 5.4 broadcast_select_fusion.3
  24.4 2.0 gather_fusion.2
  26.4 2.0 gather_fusion.1
  28.4 2.0 gather_fusion.3
  30.4 2.0 gather_fusion.4
  32.4 2.0 gather_fusion
  34.5 2.7 fusion.3
  40.0 0.8 copy-done.4
  42.4 1.6 add_convert_fusion
  44.0 1.3 fusion.15
  45.3 1.1 copy.27
  46.6 44.8 %all_gather.8 = f32[512,128]{1,0:T(8,128)S(1)} all-gather(f32[64,128]{1,0:T(8,128)S(1)} %copy-done.12), channel_id=2, replica_groups=mesh['dof'=64,'real'=8] {'real'}, dimensions={0}, use_global_device_ids=true | all-gather | bytes 294912 | tf_op jit(solution)/shard_map/all_gather | solution.py:108
  91.5 492.6 %all-reduce.4.cloned.1.call-done = f32[4,64,512]{2,0,1:T(4,128)} async-done(((f32[4,64,512]{2,0,1:T(4,128)}), f32[4,64,512]{2,0,1:T(4,128)}) %all-reduce.4.cloned.1.call-update) | async-done | bytes 524304 | tf_op jit(solution)/shard_map/psum | solution.py:88
  584.2 2.1 fusion.14
  586.7 1.0 fusion.61
  588.0 125.4 %all-reduce.6.cloned.1.call-done = f32[2,128,128]{1,2,0:T(8,128)} async-done(((f32[2,128,128]{1,2,0:T(8,128)}), f32[2,128,128]{1,2,0:T(8,128)}) %all-reduce.6.cloned.1.call-update) | async-done | bytes 131088 | tf_op jit(solution)/shard_map/psum | solution.py:66
  713.4 0.9 broadcast_multiply_fusion.1
  714.4 0.9 fusion.48
  715.4 23.5 %custom-call.8 = f32[2,128,128]{2,1,0:T(8,128)S(1)} custom-call(f32[2,128,128]{2,1,0:T(8,128)S(1)} %fusion.48), custom_call_target="Cholesky" | custom-call | tf_op jit(solution)/shard_map/jit(cholesky)/cholesky | solution.py:54
  739.1 19.7 %custom-call.9 = f32[2,1,128,128]{2,3,1,0:T(8,128)S(1)} custom-call(f32[2,1,128,128]{3,2,1,0:T(8,128)S(1)} %select_bitcast_fusion.1), custom_call_target="InvertDiagBlocksLowerTriangular" | custom-call | tf_op jit(solution)/shard_map/triangular_solve/custom-call.0 | solution.py:59
  759.5 45.8 %all_gather.7 = f32[2,512,128]{2,1,0:T(8,128)S(1)} all-gather(f32[2,64,128]{2,1,0:T(8,128)S(1)} %fusion.62), channel_id=1, replica_groups=mesh['dof'=64,'real'=8] {'real'}, dimensions={1}, use_global_device_ids=true | all-gather | bytes 589824 | tf_op jit(solution)/shard_map/all_gather | solution.py:108
  805.8 1.0 fusion.63
  806.9 1.0 copy.34
  807.8 106.3 %all-reduce.8.cloned.1.call-done = f32[2,128,128]{1,2,0:T(8,128)} async-done(((f32[2,128,128]{1,2,0:T(8,128)}), f32[2,128,128]{1,2,0:T(8,128)}) %all-reduce.8.cloned.1.call-update) | async-done | bytes 131088 | tf_op jit(solution)/shard_map/psum | solution.py:66
  914.1 0.9 broadcast_multiply_fusion
  915.1 0.9 fusion.45
  916.0 23.5 %custom-call.10 = f32[2,128,128]{2,1,0:T(8,128)S(1)} custom-call(f32[2,128,128]{2,1,0:T(8,128)S(1)} %fusion.45), custom_call_target="Cholesky" | custom-call | tf_op jit(solution)/shard_map/jit(cholesky)/cholesky | solution.py:54
  939.8 19.7 %custom-call.11 = f32[2,1,128,128]{2,3,1,0:T(8,128)S(1)} custom-call(f32[2,1,128,128]{3,2,1,0:T(8,128)S(1)} %select_bitcast_fusion), custom_call_target="InvertDiagBlocksLowerTriangular" | custom-call | tf_op jit(solution)/shard_map/triangular_solve/custom-call.0 | solution.py:59
  959.8 1.0 fusion.64
  (62 shorter events, 10.0 us)
Async XLA Ops:
  7.2 577.0 %copy-start = (f32[2,4]{1,0:T(2,128)S(1)}, f32[2,4]{1,0:T(2,128)}, u32[]{:S(2)}) copy-start(f32[2,4]{1,0:T(2,128)} %param.17) | copy-start | bytes 100
  7.2 577.0 %all-reduce.4.cloned.1.call-start = ((), (), s32[]{:S(2)}) async-start(), calls=%async_computation | async-start | bytes 1048576 | tf_op jit(solution)/shard_map/psum | solution.py:88
  8.3 15.9 %collective-permute-start = (bf16[256,512]{1,0:T(8,128)(2,1)S(1)}, bf16[256,512]{1,0:T(8,128)(2,1)S(1)}, u32[]{:S(2)}, u32[]{:S(2)}) collective-permute-start(bf16[256,512]{1,0:T(8,128)(2,1)S(1)} %get-tuple-element.23), channel_id=1, source_target_pairs={{0,8},{8,16},{16,24},{24,32},{32,40},{40,48},{48,56},{56,64},{64,7... | collective-permute-start | bytes 786440 | tf_op jit(solution)/shard_map/ppermute | solution.py:17
  10.2 14.0 %collective-permute-start.1 = (bf16[256,512]{1,0:T(8,128)(2,1)S(1)}, bf16[256,512]{1,0:T(8,128)(2,1)S(1)}, u32[]{:S(2)}, u32[]{:S(2)}) collective-permute-start(bf16[256,512]{1,0:T(8,128)(2,1)S(1)} %get-tuple-element.24), channel_id=1, source_target_pairs={{8,0},{16,8},{24,16},{32,24},{40,32},{48,40},{56,48},{64,56},{72,6... | collective-permute-start | bytes 786440 | tf_op jit(solution)/shard_map/ppermute | solution.py:20
  18.0 6.2 copy-start.5
  34.5 2.7 copy-start.3
  34.5 3.2 copy-start.6
  37.6 1.6 copy-start.2
  39.2 1.6 copy-start.4
  40.8 1.6 copy-start.1
  42.4 1.6 copy-start.8
  42.4 1.6 copy-start.9
  42.4 1.6 copy-start.10
  42.4 1.6 copy-start.11
  44.0 2.5 copy-start.12
  46.5 666.9 %all-reduce.6.cloned.1.call-start = ((), (), s32[]{:S(2)}) async-start(), calls=%async_computation.1 | async-start | bytes 262144 | tf_op jit(solution)/shard_map/psum | solution.py:66
  586.7 220.2 %copy-start.7 = (f32[4,64,512]{2,0,1:T(4,128)S(1)}, f32[4,64,512]{2,0,1:T(4,128)}, u32[]{:S(2)}) copy-start(f32[4,64,512]{2,0,1:T(4,128)} %all-reduce.4.cloned.1.call-done) | copy-start | bytes 1572868
  587.8 326.3 %all-reduce.8.cloned.1.call-start = ((), (), s32[]{:S(2)}) async-start(), calls=%async_computation.2 | async-start | bytes 262144 | tf_op jit(solution)/shard_map/psum | solution.py:66
Sparse Core Ops, SparseCore 0:
  46.6 537.4 all-reduce.3
  587.9 125.4 all-reduce.5
  807.0 107.0 all-reduce.7
where the time goes:
time: 968 us; the launch traced here: 967 us
  waiting for transfers between devices  724 us (75%)
  other arithmetic  97.6 us (10%)
  blocking collectives  90.7 us (9%)
  local copies, waits for them, and re-layouts  17.1 us (2%)
  matrix products  15 us (2%)
  between operations  14.1 us (1%)
    psum x1, waiting for transfers between devices, on_device(): summed = lax.psum(blade_parts, 'dof')  493 us
    psum x2, waiting for transfers between devices, normalize_parts(): lax.psum(partial_inner_products, 'real') / ADJUSTED_MODES  232 us
    all_gather x2, blocking collectives, on_device(): lax.all_gather(current, 'real', axis=1, tiled=True)  90.7 us
    another operation x7, other arithmetic, inverse_factor(): factor = jnp.linalg.cholesky(inner_product_matrix)  47.2 us
    another operation x5, other arithmetic, inverse_factor(): lax.linalg.triangular_solve(factor, identity, left_side=True, lower=True)  39.6 us
  transfers between devices with their start and end apart: 5, of which 3 were waited for; matrix products, arithmetic and copies ran while one was open for 1% of the time, Pallas kernels for 0%

commit v1 on v0

--- a/solution.py
+++ b/solution.py
@@ -7,6 +7,9 @@
 NBLADE = 4
 STEPS = 2
 highest_accuracy = lax.Precision.HIGHEST
+begin_the_copies = lambda packet: jnp.concatenate(
+    lax.all_to_all(jnp.stack([packet] * lax.axis_size("real")), "real", 0, 0), axis=1
+)
 
 
 def with_halo(block, sides, width):
@@ -103,10 +106,7 @@
     current = jnp.broadcast_to(start_block[None], (realizations, owned_rows, subspace_width))
     for iteration in range(STEPS):
         present_image = jnp.einsum(
-            "zjk,zks->zjs",
-            reduced,
-            lax.all_gather(current, "real", axis=1, tiled=True),
-            precision=highest_accuracy,
+            "zjk,zks->zjs", reduced, begin_the_copies(current), precision=highest_accuracy
         )
         current = normalize_parts(present_image)
     return (projected, current)

time: 968 us -> 953 us (0.985)
  blocking collectives: 90.7 us -> 17 us
  waiting for transfers between devices: 724 us -> 771 us
    all_gather x2 -> x0, blocking collectives: 90.7 us -> none  [on_device(): lax.all_gather(current, 'real', axis=1, tiled=True)]
    psum x1, waiting for transfers between devices: 493 us -> 537 us  [on_device(): summed = lax.psum(blade_parts, 'dof')]
    all_to_all x0 -> x1, blocking collectives: none -> 17 us  [lax.all_to_all(jnp.stack([packet] * lax.axis_size('real')), 'real', 0, 0)]
  transfers between devices with their start and end apart: 5 -> 6, of which waited for: 3 -> 3; matrix products, arithmetic and copies ran while one was open for 1% -> 3% of each run, Pallas kernels for 0% -> 0%
where the time goes in v1:
time: 953 us; the launch traced here: 952 us
  waiting for transfers between devices  771 us (81%)
  other arithmetic  97.7 us (10%)
  local copies, waits for them, and re-layouts  18.9 us (2%)
  starting transfers between devices  18.1 us (2%)
  blocking collectives  17 us (2%)
  matrix products  15.1 us (2%)
  between operations  14.1 us (1%)
    psum x1, waiting for transfers between devices, on_device(): summed = lax.psum(blade_parts, 'dof')  537 us
    psum x2, waiting for transfers between devices, normalize_parts(): lax.psum(partial_inner_products, 'real') / ADJUSTED_MODES  234 us
    another operation x7, other arithmetic, inverse_factor(): factor = jnp.linalg.cholesky(inner_product_matrix)  47.2 us
    another operation x5, other arithmetic, inverse_factor(): lax.linalg.triangular_solve(factor, identity, left_side=True, lower=True)  39.6 us
  transfers between devices with their start and end apart: 6, of which 3 were waited for; matrix products, arithmetic and copies ran while one was open for 3% of the time, Pallas kernels for 0%

profile of v1, /device:TPU:64, one launch (start us, length us, event | category | flops | bytes accessed | tf_op | source)
XLA Modules:
  0.0 952.2 jit_solution(187412741088649045)
XLA Ops:
  7.2 1.1 fusion.59
  8.3 1.9 collective-permute-start
  10.2 6.3 collective-permute-start.1
  16.6 1.6 stack.4
  18.2 9.6 %all-to-all-start = ((f32[8,2,64,128]{3,2,1,0:T(8,128)}), f32[8,2,64,128]{3,2,1,0:T(8,128)S(1)}, u32[]{:S(2)}, u32[]{:S(2)}) async-start(f32[8,2,64,128]{3,2,1,0:T(8,128)} %stack.4), calls=%async_computation | async-start | bytes 1048576 | tf_op jit(solution)/shard_map/all_to_all | solution.py:11
  27.9 5.3 broadcast_select_fusion.3
  33.2 1.9 pad_maximum_fusion
  35.0 2.0 gather_fusion.2
  37.0 2.0 gather_fusion.1
  39.1 2.0 gather_fusion.3
  41.1 2.0 gather_fusion.4
  43.1 2.0 gather_fusion
  45.1 2.7 fusion.3
  53.1 1.6 add_convert_fusion
  54.7 1.3 fusion.15
  56.0 1.1 copy.42
  58.1 536.8 %all-reduce.4.cloned.1.call-done = f32[4,64,512]{2,0,1:T(4,128)} async-done(((f32[4,64,512]{2,0,1:T(4,128)}), f32[4,64,512]{2,0,1:T(4,128)}) %all-reduce.4.cloned.1.call-update) | async-done | bytes 524304 | tf_op jit(solution)/shard_map/psum | solution.py:91
  594.8 2.1 fusion.14
  597.4 1.0 fusion.60
  598.8 125.4 %all-reduce.6.cloned.1.call-done = f32[2,128,128]{1,2,0:T(8,128)} async-done(((f32[2,128,128]{1,2,0:T(8,128)}), f32[2,128,128]{1,2,0:T(8,128)}) %all-reduce.6.cloned.1.call-update) | async-done | bytes 131088 | tf_op jit(solution)/shard_map/psum | solution.py:69
  724.2 0.9 broadcast_multiply_fusion.1
  725.2 0.9 fusion.47
  726.1 23.5 %custom-call.8 = f32[2,128,128]{2,1,0:T(8,128)S(1)} custom-call(f32[2,128,128]{2,1,0:T(8,128)S(1)} %fusion.47), custom_call_target="Cholesky" | custom-call | tf_op jit(solution)/shard_map/jit(cholesky)/cholesky | solution.py:57
  749.8 19.7 %custom-call.9 = f32[2,1,128,128]{2,3,1,0:T(8,128)S(1)} custom-call(f32[2,1,128,128]{3,2,1,0:T(8,128)S(1)} %select_bitcast_fusion.1), custom_call_target="InvertDiagBlocksLowerTriangular" | custom-call | tf_op jit(solution)/shard_map/triangular_solve/custom-call.0 | solution.py:62
  770.3 17.0 %all_to_all.10 = f32[8,2,64,128]{3,2,1,0:T(8,128)S(1)} all-to-all(f32[8,2,64,128]{3,2,1,0:T(8,128)S(1)} %stack.5), channel_id=1, replica_groups=mesh['dof'=64,'real'=8] {'real'}, dimensions={0} | all-to-all | bytes 1048576 | tf_op jit(solution)/shard_map/all_to_all | solution.py:11
  787.8 1.0 fusion.62
  788.9 1.0 copy.53
  789.8 109.1 %all-reduce.8.cloned.1.call-done = f32[2,128,128]{1,2,0:T(8,128)} async-done(((f32[2,128,128]{1,2,0:T(8,128)}), f32[2,128,128]{1,2,0:T(8,128)}) %all-reduce.8.cloned.1.call-update) | async-done | bytes 131088 | tf_op jit(solution)/shard_map/psum | solution.py:69
  900.0 0.9 fusion.44
  900.9 23.5 %custom-call.10 = f32[2,128,128]{2,1,0:T(8,128)S(1)} custom-call(f32[2,128,128]{2,1,0:T(8,128)S(1)} %fusion.44), custom_call_target="Cholesky" | custom-call | tf_op jit(solution)/shard_map/jit(cholesky)/cholesky | solution.py:57
  924.6 19.7 %custom-call.11 = f32[2,1,128,128]{2,3,1,0:T(8,128)S(1)} custom-call(f32[2,1,128,128]{3,2,1,0:T(8,128)S(1)} %select_bitcast_fusion), custom_call_target="InvertDiagBlocksLowerTriangular" | custom-call | tf_op jit(solution)/shard_map/triangular_solve/custom-call.0 | solution.py:62
  944.7 1.0 fusion.63
  (67 shorter events, 10.3 us)
Async XLA Ops:
  7.2 587.7 %copy-start = (f32[2,4]{1,0:T(2,128)S(1)}, f32[2,4]{1,0:T(2,128)}, u32[]{:S(2)}) copy-start(f32[2,4]{1,0:T(2,128)} %param.17) | copy-start | bytes 100
  7.2 20.6 %copy-start.12 = (s32[16,5]{0,1:T(8,128)S(1)}, s32[16,5]{0,1:T(8,128)}, u32[]{:S(2)}) copy-start(s32[16,5]{0,1:T(8,128)} %param.14) | copy-start | bytes 964
  7.2 20.6 %copy-start.11 = (s32[2048]{0:T(1024)S(1)}, s32[2048]{0:T(1024)}, u32[]{:S(2)}) copy-start(s32[2048]{0:T(1024)} %param.15) | copy-start | bytes 24580
  8.3 24.9 %collective-permute-start = (bf16[256,512]{1,0:T(8,128)(2,1)S(1)}, bf16[256,512]{1,0:T(8,128)(2,1)S(1)}, u32[]{:S(2)}, u32[]{:S(2)}) collective-permute-start(bf16[256,512]{1,0:T(8,128)(2,1)S(1)} %get-tuple-element.25), channel_id=1, source_target_pairs={{0,8},{8,16},{16,24},{24,32},{32,40},{40,48},{48,56},{56,64},{64,7... | collective-permute-start | bytes 786440 | tf_op jit(solution)/shard_map/ppermute | solution.py:20
  10.2 23.0 %collective-permute-start.1 = (bf16[256,512]{1,0:T(8,128)(2,1)S(1)}, bf16[256,512]{1,0:T(8,128)(2,1)}, u32[]{:S(2)}, u32[]{:S(2)}) collective-permute-start(bf16[256,512]{1,0:T(8,128)(2,1)S(1)} %get-tuple-element.26), channel_id=1, source_target_pairs={{8,0},{16,8},{24,16},{32,24},{40,32},{48,40},{56,48},{64,56},{72,6... | collective-permute-start | bytes 786440 | tf_op jit(solution)/shard_map/ppermute | solution.py:23
  18.2 578.8 %all-to-all-start = ((f32[8,2,64,128]{3,2,1,0:T(8,128)}), f32[8,2,64,128]{3,2,1,0:T(8,128)S(1)}, u32[]{:S(2)}, u32[]{:S(2)}) async-start(f32[8,2,64,128]{3,2,1,0:T(8,128)} %stack.4), calls=%async_computation | async-start | bytes 1048576 | tf_op jit(solution)/shard_map/all_to_all | solution.py:11
  27.7 567.1 %all-reduce.4.cloned.1.call-start = ((), (), s32[]{:S(2)}) async-start(), calls=%async_computation.2 | async-start | bytes 1048576 | tf_op jit(solution)/shard_map/psum | solution.py:91
  45.1 2.7 copy-start.3
  45.1 3.2 copy-start.5
  48.3 1.6 copy-start.2
  49.9 1.6 copy-start.4
  51.5 1.6 copy-start.1
  53.1 1.6 copy-start.7
  53.1 1.6 copy-start.8
  53.1 1.6 copy-start.9
  53.1 1.6 copy-start.10
  57.1 667.0 %all-reduce.6.cloned.1.call-start = ((), (), s32[]{:S(2)}) async-start(), calls=%async_computation.3 | async-start | bytes 262144 | tf_op jit(solution)/shard_map/psum | solution.py:69
  598.5 300.4 %all-reduce.8.cloned.1.call-start = ((), (), s32[]{:S(2)}) async-start(), calls=%async_computation.4 | async-start | bytes 262144 | tf_op jit(solution)/shard_map/psum | solution.py:69
  769.9 19.0 %copy-start.6 = (f32[4,64,512]{2,0,1:T(4,128)S(1)}, f32[4,64,512]{2,0,1:T(4,128)}, u32[]{:S(2)}) copy-start(f32[4,64,512]{2,0,1:T(4,128)} %all-reduce.4.cloned.1.call-done) | copy-start | bytes 1572868
Sparse Core Ops, SparseCore 0:
  57.3 537.5 all-reduce.3
  598.6 125.4 all-reduce.5
  789.0 109.9 all-reduce.7
